TPU v7x, 512 devices: a whole 4x8x8 slice. The times are simulated.
512 devices in a mesh: blk: 64 (over y_lo, z, x), row: 8 (over y_hi, core).
Axes of the slice: x: 4, y: 8 (y_hi: 4, y_lo: 2; y = y_hi * 2 + y_lo), z: 8, core: 2. Of those that a mesh axis runs over, the one named last changes fastest.
Arguments:
- points: bfloat16 [65536, 128], P(('blk', 'row')), may hold values from -6 to 6
- w_in: bfloat16 [128, 1024], replicated, may hold values from -0.5 to 0.5
- b_in: float32 [1024], replicated, may hold values from -4 to 4
- w_out: bfloat16 [1024, 128], replicated, may hold values from -0.1875 to 0.1875
- scales: float32 [128], replicated, may hold values from 0.04 to 0.16
- left: bfloat16 [65536, 64], P(('blk', 'row')), may hold values from -2 to 2
- right: bfloat16 [65536, 64], P(('blk', 'row')), may hold values from -2 to 2
Outputs:
- feat_grad: float32 [65536, 128], P(('blk', 'row'))
- grad_w_in: float32 [128, 1024], replicated
- grad_b_in: float32 [1024], replicated
- grad_w_out: float32 [1024, 128], replicated
All inputs are finite; a program needn't handle non-finite values.
Results may differ from a plain program's by a relative error of at most 0.012.
The roundings to bfloat16 on the way count: a program that leaves them out, or rounds other values in their place, can miss the bound.
Values may be sent and summed in bfloat16 or wider, within the bound.
A program may use at most 64 MiB of HBM per device.

v0:
```python
import jax
import jax.numpy as jnp
from jax import lax
from jax.sharding import PartitionSpec as P


def sent_together(arrays, axis, dim, along):
    widths = [a.shape[along] for a in arrays]
    both = jnp.concatenate(arrays, axis=along)
    result = lax.all_gather(both, axis, axis=dim, tiled=True)
    return tuple(jnp.split(result, [sum(widths[:k]) for k in range(1, len(widths))], axis=along))


def from_behind(value, axis, steps):
    count = lax.axis_size(axis)
    pairs = [(source, (source + steps) % count) for source in range(count)]
    return lax.ppermute(value, axis, pairs)


def cut_along(array, dim, devices):
    lengths = array.shape
    blocks = array.reshape(*lengths[:dim], devices, lengths[dim] // devices, *lengths[dim + 1 :])
    return jnp.moveaxis(blocks, dim, 0)


def sum_at_owner(array, axis, dim):
    blocks = cut_along(array, dim, lax.axis_size(axis))
    arrived = lax.all_to_all(blocks, axis, split_axis=0, concat_axis=0, tiled=True)
    return arrived.sum(axis=0)


def silu_slope(pre):
    sig = jax.nn.sigmoid(pre)
    return sig * (1.0 + pre * (1.0 - sig))


def local(points, w_in, b_in, w_out, scales, left, right):
    pre = jnp.dot(points, w_in, preferred_element_type=jnp.float32) + b_in
    hidden = jax.nn.silu(pre).astype(jnp.bfloat16)
    feats = jnp.dot(hidden, w_out, preferred_element_type=jnp.float32)
    scaled = (feats * scales).astype(jnp.bfloat16)
    pairs_ab = jnp.concatenate([left, right], axis=1)
    pairs_ba = jnp.concatenate([right, left], axis=1)
    home_g, home_ab = sent_together((scaled, pairs_ab), "row", 0, 1)
    home_f = home_g.astype(jnp.float32)
    home_n = jnp.sum(home_f * home_f, axis=1)
    contract = (((1,), (1,)), ((), ()))
    down = (((0,), (0,)), ((), ()))

    def tile(visit_g, visit_ba):
        visit_f = visit_g.astype(jnp.float32)
        visit_n = jnp.sum(visit_f * visit_f, axis=1)
        cross = lax.dot_general(visit_g, home_g, contract, preferred_element_type=jnp.float32)
        kern = jnp.exp(-0.5 * (visit_n[:, None] + home_n[None, :] - 2.0 * cross))
        coup = lax.dot_general(visit_ba, home_ab, contract, preferred_element_type=jnp.float32)
        weight = coup * kern
        weight_b = weight.astype(jnp.bfloat16)
        home_term = -jnp.sum(weight, axis=0)[:, None] * home_f + lax.dot_general(
            weight_b, visit_g, down, preferred_element_type=jnp.float32
        )
        visit_term = -jnp.sum(weight, axis=1)[:, None] * visit_f + jnp.dot(
            weight_b, home_g, preferred_element_type=jnp.float32
        )
        return (home_term, visit_term)

    home_acc, unused = tile(scaled, pairs_ba)
    blocks = lax.axis_size("blk")
    half = blocks // 2

    def visit_step(step, carry):
        visit_g, visit_ba, visit_acc, total = carry
        visit_g, visit_ba, visit_acc = (
            from_behind(visit_g.astype(jnp.float32), "blk", 1).astype(visit_g.dtype),
            from_behind(visit_ba.astype(jnp.float32), "blk", 1).astype(visit_ba.dtype),
            from_behind(visit_acc, "blk", 1),
        )
        home_term, visit_term = tile(visit_g, visit_ba)
        keep = (step < half).astype(jnp.float32)
        return (visit_g, visit_ba, visit_acc + keep * visit_term, total + home_term)

    start = (scaled, pairs_ba, jnp.zeros(feats.shape, jnp.float32), home_acc)
    unused_g, unused_ba, visit_acc, home_acc = lax.fori_loop(1, half + 1, visit_step, start)
    carried = from_behind(visit_acc, "blk", -half)
    own_sum = sum_at_owner(home_acc, "row", 0)
    feat_grad = (own_sum + carried) * scales
    feat_grad_b = feat_grad.astype(jnp.bfloat16)
    part_w_out = jnp.dot(hidden.T, feat_grad_b, preferred_element_type=jnp.float32)
    pre_grad = jnp.dot(feat_grad_b, w_out.T, preferred_element_type=jnp.float32) * silu_slope(pre)
    pre_grad_b = pre_grad.astype(jnp.bfloat16)
    part_w_in = jnp.dot(points.T, pre_grad_b, preferred_element_type=jnp.float32)
    part_b_in = jnp.sum(pre_grad, axis=0)
    grad_w_in, grad_b_in, grad_w_out = lax.psum((part_w_in, part_b_in, part_w_out), ("blk", "row"))
    factor = (points.shape[0] * blocks * lax.axis_size("row")) ** (-0.5)
    return (feat_grad, factor * grad_w_in, factor * grad_b_in, factor * grad_w_out)


def solution(mesh):
    placed = (
        P(("blk", "row"), None),
        P(),
        P(),
        P(),
        P(),
        P(("blk", "row"), None),
        P(("blk", "row"), None),
    )
    return jax.shard_map(
        local,
        mesh=mesh,
        in_specs=placed,
        out_specs=(P(("blk", "row"), None), P(), P(), P()),
        check_vma=False,
    )
```

profile of v0, /device:TPU:23, one launch (start us, length us, event | category | flops | bytes accessed | tf_op | source)
XLA Modules:
  0.0 814.2 jit_solution(11493214395384115716)
XLA Ops:
  10.8 16.0 %all_gather.3 = bf16[1024,256]{0,1:T(8,128)(2,1)S(1)} all-gather(bf16[128,256]{0,1:T(8,128)(2,1)S(1)} %pad_maximum_fusion), channel_id=1, replica_groups=mesh['blk'=64,'row'=8] {'row'}, dimensions={0}, use_global_device_ids=true | all-gather | bytes 589824 | tf_op jit(solution)/shard_map/all_gather | solution.py:10
  29.5 429.8 %while.20 = (s32[]{:T(128)}, bf16[128,128]{1,0:T(8,128)(2,1)S(1)}, bf16[128,128]{1,0:T(8,128)(2,1)S(1)}, f32[128,128]{1,0:T(8,128)S(1)}, f32[1024,128]{1,0:T(8,1...) while((s32[]{:T(128)}, bf16[128,128]{1,0:T(8,128)(2,1)S(1)}, ...), condition=%wide.region_7.8_spmd.clone, body=%wide.region_3.7_spmd.clone.sunk | while | flops 135806848 | bytes 5299465 | solution.py:82
  29.5 3.9 collective-permute-start
  33.4 3.1 collective-permute-start.1
  36.6 3.1 collective-permute-start.2
  42.8 4.2 collective-permute-start
  49.6 3.1 collective-permute-start.2
  55.9 4.2 collective-permute-start
  60.1 3.1 collective-permute-start.1
  69.1 4.2 collective-permute-start
  76.3 3.1 collective-permute-start.2
  82.6 4.2 collective-permute-start
  86.8 3.8 collective-permute-start.1
  90.6 3.1 collective-permute-start.2
  96.8 4.3 collective-permute-start
  101.2 4.5 collective-permute-start.1
  111.3 4.2 collective-permute-start
  115.5 3.2 collective-permute-start.1
  124.5 3.8 collective-permute-start
  136.6 4.7 collective-permute-start
  149.0 4.2 collective-permute-start
  153.3 3.1 collective-permute-start.1
  162.6 4.5 collective-permute-start
  175.0 4.2 collective-permute-start
  179.2 3.1 collective-permute-start.1
  187.6 4.7 collective-permute-start
  200.3 4.2 collective-permute-start
  204.5 3.5 collective-permute-start.1
  213.5 4.2 collective-permute-start
  217.8 4.2 collective-permute-start.1
  227.3 4.6 collective-permute-start
  231.9 3.4 collective-permute-start.1
  241.1 4.6 collective-permute-start
  245.7 3.4 collective-permute-start.1
  254.3 4.6 collective-permute-start
  258.9 4.0 collective-permute-start.1
  268.8 4.8 collective-permute-start
  281.8 3.6 collective-permute-start
  285.4 4.5 collective-permute-start.1
  295.6 3.8 collective-permute-start
  299.4 4.8 collective-permute-start.1
  309.5 4.2 collective-permute-start
  322.5 4.2 collective-permute-start
  326.7 4.0 collective-permute-start.1
  336.0 4.8 collective-permute-start
  340.8 4.0 collective-permute-start.1
  350.4 4.2 collective-permute-start
  354.6 4.0 collective-permute-start.1
  364.0 5.0 collective-permute-start
  371.7 3.1 collective-permute-start.2
  378.0 4.2 collective-permute-start
  382.2 3.6 collective-permute-start.1
  391.1 4.2 collective-permute-start
  395.3 4.3 collective-permute-start.1
  405.2 4.5 collective-permute-start
  418.2 4.2 collective-permute-start
  422.4 4.2 collective-permute-start.1
  432.0 4.2 collective-permute-start
  436.2 4.1 collective-permute-start.1
  446.2 4.5 collective-permute-start
  459.3 44.4 %all-to-all-start = ((f32[8,128,128]{2,1,0:T(8,128)}), f32[8,128,128]{2,1,0:T(8,128)S(1)}, u32[]{:S(2)}, u32[]{:S(2)}) async-start(f32[8,128,128]{2,1,0:T(8,128)} %bitcast), calls=%async_computation | async-start | bytes 1048576 | tf_op jit(solution)/shard_map/all_to_all | solution.py:28
  506.8 7.9 all-to-all-done
  520.9 106.4 %psum.22 = f32[1024]{0:T(1024)S(1)} all-reduce(f32[1024]{0:T(1024)S(1)} %get-tuple-element.247), channel_id=1, replica_groups=mesh['blk'=64,'row'=8] {'blk','row'}, use_global_device_ids=true, to_apply=%region_11.12 | all-reduce | flops 1024 | bytes 8192 | tf_op jit(solution)/shard_map/psum | solution.py:92
  627.9 176.5 %all-reduce.3.cloned.1.call-done = (f32[128,1024]{0,1:T(8,128)}, f32[1024,128]{1,0:T(8,128)}) async-done(((f32[128,1024]{0,1:T(8,128)}, f32[1024,128]{1,0:T(8,128)}), (f32[128,1024]{0,1:T(8,128)}, f32[1024,128]{1,0:T(8,128)})) %all-reduce.3.cloned.1.call-update) | async-done | bytes 1048592 | tf_op jit(solution)/shard_map/psum | solution.py:92
  (502 shorter events, 211.5 us)
Async XLA Ops:
  29.5 10.2 %collective-permute-start = (bf16[128,128]{1,0:T(8,128)(2,1)S(1)}, bf16[128,128]{1,0:T(8,128)(2,1)S(1)}, u32[]{:S(2)}, u32[]{:S(2)}) collective-permute-start(bf16[128,128]{1,0:T(8,128)(2,1)S(1)} %get-tuple-element.330), channel_id=1, source_target_pairs={{0,8},{8,16},{16,24},{24,32},{32,40},{40,48},{48,56},{56,64},{64,7... | collective-permute-start | bytes 98312 | tf_op jit(solution)/shard_map/while/body/eval_jaxpr/ppermute | solution.py:17
  33.4 6.7 collective-permute-start.1
  36.6 6.0 collective-permute-start.2
  42.8 9.9 %collective-permute-start = (bf16[128,128]{1,0:T(8,128)(2,1)S(1)}, bf16[128,128]{1,0:T(8,128)(2,1)S(1)}, u32[]{:S(2)}, u32[]{:S(2)}) collective-permute-start(bf16[128,128]{1,0:T(8,128)(2,1)S(1)} %get-tuple-element.330), channel_id=1, source_target_pairs={{0,8},{8,16},{16,24},{24,32},{32,40},{40,48},{48,56},{56,64},{64,7... | collective-permute-start | bytes 98312 | tf_op jit(solution)/shard_map/while/body/eval_jaxpr/ppermute | solution.py:17
  47.1 6.1 collective-permute-start.1
  49.6 6.0 collective-permute-start.2
  55.9 9.9 %collective-permute-start = (bf16[128,128]{1,0:T(8,128)(2,1)S(1)}, bf16[128,128]{1,0:T(8,128)(2,1)S(1)}, u32[]{:S(2)}, u32[]{:S(2)}) collective-permute-start(bf16[128,128]{1,0:T(8,128)(2,1)S(1)} %get-tuple-element.330), channel_id=1, source_target_pairs={{0,8},{8,16},{16,24},{24,32},{32,40},{40,48},{48,56},{56,64},{64,7... | collective-permute-start | bytes 98312 | tf_op jit(solution)/shard_map/while/body/eval_jaxpr/ppermute | solution.py:17
  60.1 6.1 collective-permute-start.1
  69.1 10.3 %collective-permute-start = (bf16[128,128]{1,0:T(8,128)(2,1)S(1)}, bf16[128,128]{1,0:T(8,128)(2,1)S(1)}, u32[]{:S(2)}, u32[]{:S(2)}) collective-permute-start(bf16[128,128]{1,0:T(8,128)(2,1)S(1)} %get-tuple-element.330), channel_id=1, source_target_pairs={{0,8},{8,16},{16,24},{24,32},{32,40},{40,48},{48,56},{56,64},{64,7... | collective-permute-start | bytes 98312 | tf_op jit(solution)/shard_map/while/body/eval_jaxpr/ppermute | solution.py:17
  73.3 6.5 collective-permute-start.1
  76.3 6.0 collective-permute-start.2
  82.6 11.1 %collective-permute-start = (bf16[128,128]{1,0:T(8,128)(2,1)S(1)}, bf16[128,128]{1,0:T(8,128)(2,1)S(1)}, u32[]{:S(2)}, u32[]{:S(2)}) collective-permute-start(bf16[128,128]{1,0:T(8,128)(2,1)S(1)} %get-tuple-element.330), channel_id=1, source_target_pairs={{0,8},{8,16},{16,24},{24,32},{32,40},{40,48},{48,56},{56,64},{64,7... | collective-permute-start | bytes 98312 | tf_op jit(solution)/shard_map/while/body/eval_jaxpr/ppermute | solution.py:17
  86.8 7.3 collective-permute-start.1
  90.6 6.0 collective-permute-start.2
  96.8 11.3 %collective-permute-start = (bf16[128,128]{1,0:T(8,128)(2,1)S(1)}, bf16[128,128]{1,0:T(8,128)(2,1)S(1)}, u32[]{:S(2)}, u32[]{:S(2)}) collective-permute-start(bf16[128,128]{1,0:T(8,128)(2,1)S(1)} %get-tuple-element.330), channel_id=1, source_target_pairs={{0,8},{8,16},{16,24},{24,32},{32,40},{40,48},{48,56},{56,64},{64,7... | collective-permute-start | bytes 98312 | tf_op jit(solution)/shard_map/while/body/eval_jaxpr/ppermute | solution.py:17
  101.2 7.4 collective-permute-start.1
  111.3 9.6 %collective-permute-start = (bf16[128,128]{1,0:T(8,128)(2,1)S(1)}, bf16[128,128]{1,0:T(8,128)(2,1)S(1)}, u32[]{:S(2)}, u32[]{:S(2)}) collective-permute-start(bf16[128,128]{1,0:T(8,128)(2,1)S(1)} %get-tuple-element.330), channel_id=1, source_target_pairs={{0,8},{8,16},{16,24},{24,32},{32,40},{40,48},{48,56},{56,64},{64,7... | collective-permute-start | bytes 98312 | tf_op jit(solution)/shard_map/while/body/eval_jaxpr/ppermute | solution.py:17
  124.5 8.9 %collective-permute-start = (bf16[128,128]{1,0:T(8,128)(2,1)S(1)}, bf16[128,128]{1,0:T(8,128)(2,1)S(1)}, u32[]{:S(2)}, u32[]{:S(2)}) collective-permute-start(bf16[128,128]{1,0:T(8,128)(2,1)S(1)} %get-tuple-element.330), channel_id=1, source_target_pairs={{0,8},{8,16},{16,24},{24,32},{32,40},{40,48},{48,56},{56,64},{64,7... | collective-permute-start | bytes 98312 | tf_op jit(solution)/shard_map/while/body/eval_jaxpr/ppermute | solution.py:17
  136.6 9.3 %collective-permute-start = (bf16[128,128]{1,0:T(8,128)(2,1)S(1)}, bf16[128,128]{1,0:T(8,128)(2,1)S(1)}, u32[]{:S(2)}, u32[]{:S(2)}) collective-permute-start(bf16[128,128]{1,0:T(8,128)(2,1)S(1)} %get-tuple-element.330), channel_id=1, source_target_pairs={{0,8},{8,16},{16,24},{24,32},{32,40},{40,48},{48,56},{56,64},{64,7... | collective-permute-start | bytes 98312 | tf_op jit(solution)/shard_map/while/body/eval_jaxpr/ppermute | solution.py:17
  149.0 10.1 %collective-permute-start = (bf16[128,128]{1,0:T(8,128)(2,1)S(1)}, bf16[128,128]{1,0:T(8,128)(2,1)S(1)}, u32[]{:S(2)}, u32[]{:S(2)}) collective-permute-start(bf16[128,128]{1,0:T(8,128)(2,1)S(1)} %get-tuple-element.330), channel_id=1, source_target_pairs={{0,8},{8,16},{16,24},{24,32},{32,40},{40,48},{48,56},{56,64},{64,7... | collective-permute-start | bytes 98312 | tf_op jit(solution)/shard_map/while/body/eval_jaxpr/ppermute | solution.py:17
  153.3 6.3 collective-permute-start.1
  156.4 6.0 collective-permute-start.2
  162.6 9.2 %collective-permute-start = (bf16[128,128]{1,0:T(8,128)(2,1)S(1)}, bf16[128,128]{1,0:T(8,128)(2,1)S(1)}, u32[]{:S(2)}, u32[]{:S(2)}) collective-permute-start(bf16[128,128]{1,0:T(8,128)(2,1)S(1)} %get-tuple-element.330), channel_id=1, source_target_pairs={{0,8},{8,16},{16,24},{24,32},{32,40},{40,48},{48,56},{56,64},{64,7... | collective-permute-start | bytes 98312 | tf_op jit(solution)/shard_map/while/body/eval_jaxpr/ppermute | solution.py:17
  175.0 9.5 %collective-permute-start = (bf16[128,128]{1,0:T(8,128)(2,1)S(1)}, bf16[128,128]{1,0:T(8,128)(2,1)S(1)}, u32[]{:S(2)}, u32[]{:S(2)}) collective-permute-start(bf16[128,128]{1,0:T(8,128)(2,1)S(1)} %get-tuple-element.330), channel_id=1, source_target_pairs={{0,8},{8,16},{16,24},{24,32},{32,40},{40,48},{48,56},{56,64},{64,7... | collective-permute-start | bytes 98312 | tf_op jit(solution)/shard_map/while/body/eval_jaxpr/ppermute | solution.py:17
  187.6 9.6 %collective-permute-start = (bf16[128,128]{1,0:T(8,128)(2,1)S(1)}, bf16[128,128]{1,0:T(8,128)(2,1)S(1)}, u32[]{:S(2)}, u32[]{:S(2)}) collective-permute-start(bf16[128,128]{1,0:T(8,128)(2,1)S(1)} %get-tuple-element.330), channel_id=1, source_target_pairs={{0,8},{8,16},{16,24},{24,32},{32,40},{40,48},{48,56},{56,64},{64,7... | collective-permute-start | bytes 98312 | tf_op jit(solution)/shard_map/while/body/eval_jaxpr/ppermute | solution.py:17
  200.3 10.0 %collective-permute-start = (bf16[128,128]{1,0:T(8,128)(2,1)S(1)}, bf16[128,128]{1,0:T(8,128)(2,1)S(1)}, u32[]{:S(2)}, u32[]{:S(2)}) collective-permute-start(bf16[128,128]{1,0:T(8,128)(2,1)S(1)} %get-tuple-element.330), channel_id=1, source_target_pairs={{0,8},{8,16},{16,24},{24,32},{32,40},{40,48},{48,56},{56,64},{64,7... | collective-permute-start | bytes 98312 | tf_op jit(solution)/shard_map/while/body/eval_jaxpr/ppermute | solution.py:17
  204.5 6.2 collective-permute-start.1
  213.5 10.6 %collective-permute-start = (bf16[128,128]{1,0:T(8,128)(2,1)S(1)}, bf16[128,128]{1,0:T(8,128)(2,1)S(1)}, u32[]{:S(2)}, u32[]{:S(2)}) collective-permute-start(bf16[128,128]{1,0:T(8,128)(2,1)S(1)} %get-tuple-element.330), channel_id=1, source_target_pairs={{0,8},{8,16},{16,24},{24,32},{32,40},{40,48},{48,56},{56,64},{64,7... | collective-permute-start | bytes 98312 | tf_op jit(solution)/shard_map/while/body/eval_jaxpr/ppermute | solution.py:17
  217.8 6.8 collective-permute-start.1
  227.3 10.7 %collective-permute-start = (bf16[128,128]{1,0:T(8,128)(2,1)S(1)}, bf16[128,128]{1,0:T(8,128)(2,1)S(1)}, u32[]{:S(2)}, u32[]{:S(2)}) collective-permute-start(bf16[128,128]{1,0:T(8,128)(2,1)S(1)} %get-tuple-element.330), channel_id=1, source_target_pairs={{0,8},{8,16},{16,24},{24,32},{32,40},{40,48},{48,56},{56,64},{64,7... | collective-permute-start | bytes 98312 | tf_op jit(solution)/shard_map/while/body/eval_jaxpr/ppermute | solution.py:17
  231.9 6.5 collective-permute-start.1
  241.1 10.1 %collective-permute-start = (bf16[128,128]{1,0:T(8,128)(2,1)S(1)}, bf16[128,128]{1,0:T(8,128)(2,1)S(1)}, u32[]{:S(2)}, u32[]{:S(2)}) collective-permute-start(bf16[128,128]{1,0:T(8,128)(2,1)S(1)} %get-tuple-element.330), channel_id=1, source_target_pairs={{0,8},{8,16},{16,24},{24,32},{32,40},{40,48},{48,56},{56,64},{64,7... | collective-permute-start | bytes 98312 | tf_op jit(solution)/shard_map/while/body/eval_jaxpr/ppermute | solution.py:17
  245.7 5.9 collective-permute-start.1
  254.3 11.3 %collective-permute-start = (bf16[128,128]{1,0:T(8,128)(2,1)S(1)}, bf16[128,128]{1,0:T(8,128)(2,1)S(1)}, u32[]{:S(2)}, u32[]{:S(2)}) collective-permute-start(bf16[128,128]{1,0:T(8,128)(2,1)S(1)} %get-tuple-element.330), channel_id=1, source_target_pairs={{0,8},{8,16},{16,24},{24,32},{32,40},{40,48},{48,56},{56,64},{64,7... | collective-permute-start | bytes 98312 | tf_op jit(solution)/shard_map/while/body/eval_jaxpr/ppermute | solution.py:17
  258.9 7.1 collective-permute-start.1
  268.8 9.3 %collective-permute-start = (bf16[128,128]{1,0:T(8,128)(2,1)S(1)}, bf16[128,128]{1,0:T(8,128)(2,1)S(1)}, u32[]{:S(2)}, u32[]{:S(2)}) collective-permute-start(bf16[128,128]{1,0:T(8,128)(2,1)S(1)} %get-tuple-element.330), channel_id=1, source_target_pairs={{0,8},{8,16},{16,24},{24,32},{32,40},{40,48},{48,56},{56,64},{64,7... | collective-permute-start | bytes 98312 | tf_op jit(solution)/shard_map/while/body/eval_jaxpr/ppermute | solution.py:17
  281.8 10.3 %collective-permute-start = (bf16[128,128]{1,0:T(8,128)(2,1)S(1)}, bf16[128,128]{1,0:T(8,128)(2,1)S(1)}, u32[]{:S(2)}, u32[]{:S(2)}) collective-permute-start(bf16[128,128]{1,0:T(8,128)(2,1)S(1)} %get-tuple-element.330), channel_id=1, source_target_pairs={{0,8},{8,16},{16,24},{24,32},{32,40},{40,48},{48,56},{56,64},{64,7... | collective-permute-start | bytes 98312 | tf_op jit(solution)/shard_map/while/body/eval_jaxpr/ppermute | solution.py:17
  285.4 7.1 collective-permute-start.1
  295.6 10.8 %collective-permute-start = (bf16[128,128]{1,0:T(8,128)(2,1)S(1)}, bf16[128,128]{1,0:T(8,128)(2,1)S(1)}, u32[]{:S(2)}, u32[]{:S(2)}) collective-permute-start(bf16[128,128]{1,0:T(8,128)(2,1)S(1)} %get-tuple-element.330), channel_id=1, source_target_pairs={{0,8},{8,16},{16,24},{24,32},{32,40},{40,48},{48,56},{56,64},{64,7... | collective-permute-start | bytes 98312 | tf_op jit(solution)/shard_map/while/body/eval_jaxpr/ppermute | solution.py:17
  299.4 7.3 collective-permute-start.1
  309.5 9.8 %collective-permute-start = (bf16[128,128]{1,0:T(8,128)(2,1)S(1)}, bf16[128,128]{1,0:T(8,128)(2,1)S(1)}, u32[]{:S(2)}, u32[]{:S(2)}) collective-permute-start(bf16[128,128]{1,0:T(8,128)(2,1)S(1)} %get-tuple-element.330), channel_id=1, source_target_pairs={{0,8},{8,16},{16,24},{24,32},{32,40},{40,48},{48,56},{56,64},{64,7... | collective-permute-start | bytes 98312 | tf_op jit(solution)/shard_map/while/body/eval_jaxpr/ppermute | solution.py:17
  313.8 5.9 collective-permute-start.1
  322.5 10.4 %collective-permute-start = (bf16[128,128]{1,0:T(8,128)(2,1)S(1)}, bf16[128,128]{1,0:T(8,128)(2,1)S(1)}, u32[]{:S(2)}, u32[]{:S(2)}) collective-permute-start(bf16[128,128]{1,0:T(8,128)(2,1)S(1)} %get-tuple-element.330), channel_id=1, source_target_pairs={{0,8},{8,16},{16,24},{24,32},{32,40},{40,48},{48,56},{56,64},{64,7... | collective-permute-start | bytes 98312 | tf_op jit(solution)/shard_map/while/body/eval_jaxpr/ppermute | solution.py:17
  326.7 6.6 collective-permute-start.1
  336.0 11.3 %collective-permute-start = (bf16[128,128]{1,0:T(8,128)(2,1)S(1)}, bf16[128,128]{1,0:T(8,128)(2,1)S(1)}, u32[]{:S(2)}, u32[]{:S(2)}) collective-permute-start(bf16[128,128]{1,0:T(8,128)(2,1)S(1)} %get-tuple-element.330), channel_id=1, source_target_pairs={{0,8},{8,16},{16,24},{24,32},{32,40},{40,48},{48,56},{56,64},{64,7... | collective-permute-start | bytes 98312 | tf_op jit(solution)/shard_map/while/body/eval_jaxpr/ppermute | solution.py:17
  340.8 6.8 collective-permute-start.1
  350.4 10.4 %collective-permute-start = (bf16[128,128]{1,0:T(8,128)(2,1)S(1)}, bf16[128,128]{1,0:T(8,128)(2,1)S(1)}, u32[]{:S(2)}, u32[]{:S(2)}) collective-permute-start(bf16[128,128]{1,0:T(8,128)(2,1)S(1)} %get-tuple-element.330), channel_id=1, source_target_pairs={{0,8},{8,16},{16,24},{24,32},{32,40},{40,48},{48,56},{56,64},{64,7... | collective-permute-start | bytes 98312 | tf_op jit(solution)/shard_map/while/body/eval_jaxpr/ppermute | solution.py:17
  354.6 6.6 collective-permute-start.1
  364.0 10.9 %collective-permute-start = (bf16[128,128]{1,0:T(8,128)(2,1)S(1)}, bf16[128,128]{1,0:T(8,128)(2,1)S(1)}, u32[]{:S(2)}, u32[]{:S(2)}) collective-permute-start(bf16[128,128]{1,0:T(8,128)(2,1)S(1)} %get-tuple-element.330), channel_id=1, source_target_pairs={{0,8},{8,16},{16,24},{24,32},{32,40},{40,48},{48,56},{56,64},{64,7... | collective-permute-start | bytes 98312 | tf_op jit(solution)/shard_map/while/body/eval_jaxpr/ppermute | solution.py:17
  368.9 6.3 collective-permute-start.1
  371.7 6.0 collective-permute-start.2
  378.0 10.0 %collective-permute-start = (bf16[128,128]{1,0:T(8,128)(2,1)S(1)}, bf16[128,128]{1,0:T(8,128)(2,1)S(1)}, u32[]{:S(2)}, u32[]{:S(2)}) collective-permute-start(bf16[128,128]{1,0:T(8,128)(2,1)S(1)} %get-tuple-element.330), channel_id=1, source_target_pairs={{0,8},{8,16},{16,24},{24,32},{32,40},{40,48},{48,56},{56,64},{64,7... | collective-permute-start | bytes 98312 | tf_op jit(solution)/shard_map/while/body/eval_jaxpr/ppermute | solution.py:17
  382.2 6.1 collective-permute-start.1
  391.1 10.7 %collective-permute-start = (bf16[128,128]{1,0:T(8,128)(2,1)S(1)}, bf16[128,128]{1,0:T(8,128)(2,1)S(1)}, u32[]{:S(2)}, u32[]{:S(2)}) collective-permute-start(bf16[128,128]{1,0:T(8,128)(2,1)S(1)} %get-tuple-element.330), channel_id=1, source_target_pairs={{0,8},{8,16},{16,24},{24,32},{32,40},{40,48},{48,56},{56,64},{64,7... | collective-permute-start | bytes 98312 | tf_op jit(solution)/shard_map/while/body/eval_jaxpr/ppermute | solution.py:17
  395.3 6.9 collective-permute-start.1
  405.2 9.8 %collective-permute-start = (bf16[128,128]{1,0:T(8,128)(2,1)S(1)}, bf16[128,128]{1,0:T(8,128)(2,1)S(1)}, u32[]{:S(2)}, u32[]{:S(2)}) collective-permute-start(bf16[128,128]{1,0:T(8,128)(2,1)S(1)} %get-tuple-element.330), channel_id=1, source_target_pairs={{0,8},{8,16},{16,24},{24,32},{32,40},{40,48},{48,56},{56,64},{64,7... | collective-permute-start | bytes 98312 | tf_op jit(solution)/shard_map/while/body/eval_jaxpr/ppermute | solution.py:17
  418.2 10.7 %collective-permute-start = (bf16[128,128]{1,0:T(8,128)(2,1)S(1)}, bf16[128,128]{1,0:T(8,128)(2,1)S(1)}, u32[]{:S(2)}, u32[]{:S(2)}) collective-permute-start(bf16[128,128]{1,0:T(8,128)(2,1)S(1)} %get-tuple-element.330), channel_id=1, source_target_pairs={{0,8},{8,16},{16,24},{24,32},{32,40},{40,48},{48,56},{56,64},{64,7... | collective-permute-start | bytes 98312 | tf_op jit(solution)/shard_map/while/body/eval_jaxpr/ppermute | solution.py:17
  422.4 6.8 collective-permute-start.1
  432.0 11.1 %collective-permute-start = (bf16[128,128]{1,0:T(8,128)(2,1)S(1)}, bf16[128,128]{1,0:T(8,128)(2,1)S(1)}, u32[]{:S(2)}, u32[]{:S(2)}) collective-permute-start(bf16[128,128]{1,0:T(8,128)(2,1)S(1)} %get-tuple-element.330), channel_id=1, source_target_pairs={{0,8},{8,16},{16,24},{24,32},{32,40},{40,48},{48,56},{56,64},{64,7... | collective-permute-start | bytes 98312 | tf_op jit(solution)/shard_map/while/body/eval_jaxpr/ppermute | solution.py:17
  436.2 7.2 collective-permute-start.1
  446.2 9.4 %collective-permute-start = (bf16[128,128]{1,0:T(8,128)(2,1)S(1)}, bf16[128,128]{1,0:T(8,128)(2,1)S(1)}, u32[]{:S(2)}, u32[]{:S(2)}) collective-permute-start(bf16[128,128]{1,0:T(8,128)(2,1)S(1)} %get-tuple-element.330), channel_id=1, source_target_pairs={{0,8},{8,16},{16,24},{24,32},{32,40},{40,48},{48,56},{56,64},{64,7... | collective-permute-start | bytes 98312 | tf_op jit(solution)/shard_map/while/body/eval_jaxpr/ppermute | solution.py:17
  459.3 55.4 %all-to-all-start = ((f32[8,128,128]{2,1,0:T(8,128)}), f32[8,128,128]{2,1,0:T(8,128)S(1)}, u32[]{:S(2)}, u32[]{:S(2)}) async-start(f32[8,128,128]{2,1,0:T(8,128)} %bitcast), calls=%async_computation | async-start | bytes 1048576 | tf_op jit(solution)/shard_map/all_to_all | solution.py:28
  503.7 300.7 %all-reduce.3.cloned.1.call-start = ((), (), s32[]{:S(2)}) async-start(), calls=%async_computation.1 | async-start | bytes 2097152 | tf_op jit(solution)/shard_map/psum | solution.py:92
  503.8 13.7 %collective-permute-start.3 = (f32[128,128]{0,1:T(8,128)S(1)}, f32[128,128]{0,1:T(8,128)S(1)}, u32[]{:S(2)}, u32[]{:S(2)}) collective-permute-start(f32[128,128]{0,1:T(8,128)S(1)} %copy.30), channel_id=1, source_target_pairs={{0,256},{8,264},{16,272},{24,280},{32,288},{40,296},{48,304},{56,3... | collective-permute-start | bytes 196616 | tf_op jit(solution)/shard_map/ppermute | solution.py:17
  (42 other events, 194.2 us)
Sparse Core Ops, SparseCore 0:
  520.3 284.1 all-reduce.2
where the time goes:
time: 819 us; the launch traced here: 814 us
  starting transfers between devices  372 us (45%)
  waiting for transfers between devices  190 us (23%)
  blocking collectives  122 us (15%)
  matrix products  99.2 us (12%)
  between operations  14.2 us (2%)
    ppermute x97, starting transfers between devices, from_behind(): return lax.ppermute(value, axis, pairs)  328 us
    psum x1, waiting for transfers between devices, local(): lax.psum((part_w_in, part_b_in, part_w_out), ('blk', 'row'))  177 us
    psum x1, blocking collectives, local(): lax.psum((part_w_in, part_b_in, part_w_out), ('blk', 'row'))  106 us
    dot_general x33, matrix products, tile(): lax.dot_general(weight_b, visit_g, down, preferred_element_type=jnp.float32)  68.8 us
    all_to_all x1, starting transfers between devices, sum_at_owner(): lax.all_to_all(blocks, axis, split_axis=0, concat_axis=0, tiled=True)  44.4 us
  transfers between devices with their start and end apart: 99, of which 10 were waited for; matrix products, arithmetic and copies ran while one was open for 11% of the time, Pallas kernels for 0%

commit v1 on v0

--- a/solution.py
+++ b/solution.py
@@ -89,7 +89,9 @@
     pre_grad_b = pre_grad.astype(jnp.bfloat16)
     part_w_in = jnp.dot(points.T, pre_grad_b, preferred_element_type=jnp.float32)
     part_b_in = jnp.sum(pre_grad, axis=0)
-    grad_w_in, grad_b_in, grad_w_out = lax.psum((part_w_in, part_b_in, part_w_out), ("blk", "row"))
+    grad_w_in, grad_b_in, grad_w_out = lax.psum(
+        lax.psum((part_w_in, part_b_in, part_w_out), "blk"), "row"
+    )
     factor = (points.shape[0] * blocks * lax.axis_size("row")) ** (-0.5)
     return (feat_grad, factor * grad_w_in, factor * grad_b_in, factor * grad_w_out)
 

time: 819 us -> 1330 us (1.62)
  the two profiles are of different devices: /device:TPU:23 before, /device:TPU:1 now
where the time goes in v1:
time: 1330 us
  waiting for transfers between devices  734 us (55%)
  blocking collectives  237 us (18%)
  starting transfers between devices  229 us (17%)
  matrix products  99.2 us (7%)
  between operations  14.3 us (1%)
    psum x1, waiting for transfers between devices, local(): lax.psum((part_w_in, part_b_in, part_w_out), 'blk')  568 us
    ppermute x97, starting transfers between devices, from_behind(): return lax.ppermute(value, axis, pairs)  190 us
    ppermute x97, waiting for transfers between devices, from_behind(): return lax.ppermute(value, axis, pairs)  153 us
    psum x1, blocking collectives, local(): lax.psum((part_w_in, part_b_in, part_w_out), 'blk')  132 us
    psum x1, blocking collectives, local(): lax.psum(lax.psum((part_w_in, part_b_in, part_w_out), 'blk'), 'row')  83.1 us
    dot_general x33, matrix products, tile(): lax.dot_general(weight_b, visit_g, down, preferred_element_type=jnp.float32)  68.8 us
    all_to_all x1, starting transfers between devices, sum_at_owner(): lax.all_to_all(blocks, axis, split_axis=0, concat_axis=0, tiled=True)  39.2 us
  transfers between devices with their start and end apart: 100, of which 73 were waited for; matrix products, arithmetic and copies ran while one was open for 7% of the time, Pallas kernels for 0%

profile of v1, /device:TPU:1, one launch (start us, length us, event | category | flops | bytes accessed | tf_op | source)
XLA Modules:
  0.0 1328.7 jit_solution(408849095584479310)
XLA Ops:
  10.8 21.6 %all_gather.3 = bf16[1024,256]{0,1:T(8,128)(2,1)S(1)} all-gather(bf16[128,256]{0,1:T(8,128)(2,1)S(1)} %pad_maximum_fusion), channel_id=1, replica_groups=mesh['blk'=64,'row'=8] {'row'}, dimensions={0}, use_global_device_ids=true | all-gather | bytes 589824 | tf_op jit(solution)/shard_map/all_gather | solution.py:10
  35.1 441.6 %while.20 = (s32[]{:T(128)}, bf16[128,128]{1,0:T(8,128)(2,1)S(1)}, bf16[128,128]{1,0:T(8,128)(2,1)S(1)}, f32[128,128]{1,0:T(8,128)S(1)}, f32[1024,128]{1,0:T(8,1...) while((s32[]{:T(128)}, bf16[128,128]{1,0:T(8,128)(2,1)S(1)}, ...), condition=%wide.region_7.8_spmd.clone, body=%wide.region_3.7_spmd.clone.sunk | while | flops 135806848 | bytes 5299465 | solution.py:82
  35.1 2.9 collective-permute-start
  38.0 3.1 collective-permute-start.1
  41.2 2.8 collective-permute-start.2
  44.0 5.3 collective-permute-done
  51.5 2.1 fusion.68
  59.9 3.1 collective-permute-done
  65.2 2.1 fusion.68
  73.5 3.1 collective-permute-done
  87.4 3.1 collective-permute-done
  92.7 2.1 fusion.68
  101.0 3.1 collective-permute-done
  106.3 2.1 fusion.68
  114.7 3.1 collective-permute-done
  120.0 2.1 fusion.68
  128.2 3.1 collective-permute-done
  133.5 2.1 fusion.68
  141.7 3.1 collective-permute-done
  147.1 2.1 fusion.68
  155.3 3.1 collective-permute-done
  160.6 2.1 fusion.68
  168.8 3.1 collective-permute-done
  174.2 2.1 fusion.68
  182.4 3.1 collective-permute-done
  187.7 2.1 fusion.68
  195.9 3.1 collective-permute-done
  199.4 2.2 collective-permute-done.1
  201.9 2.1 fusion.68
  210.1 3.4 collective-permute-done
  223.7 3.1 collective-permute-done
  229.0 2.1 fusion.68
  237.3 3.1 collective-permute-done
  250.8 3.1 collective-permute-done
  264.9 3.1 collective-permute-done
  278.4 3.1 collective-permute-done
  283.8 2.1 fusion.68
  292.1 3.1 collective-permute-done
  297.5 2.1 fusion.68
  305.7 3.1 collective-permute-done
  319.2 3.1 collective-permute-done
  324.5 2.1 fusion.68
  332.8 3.1 collective-permute-done
  346.3 3.1 collective-permute-done
  351.6 2.1 fusion.68
  359.9 3.7 collective-permute-done
  373.4 3.1 collective-permute-done
  378.7 2.1 fusion.68
  387.0 3.4 collective-permute-done
  400.5 3.1 collective-permute-done
  405.8 2.1 fusion.68
  414.1 3.1 collective-permute-done
  427.7 3.1 collective-permute-done
  441.7 3.1 collective-permute-done
  455.3 3.1 collective-permute-done
  460.6 2.1 fusion.68
  469.0 3.1 collective-permute-done
  474.3 2.1 fusion.68
  476.7 39.2 %all-to-all-start = ((f32[8,128,128]{2,1,0:T(8,128)}), f32[8,128,128]{2,1,0:T(8,128)S(1)}, u32[]{:S(2)}, u32[]{:S(2)}) async-start(f32[8,128,128]{2,1,0:T(8,128)} %bitcast), calls=%async_computation | async-start | bytes 1048576 | tf_op jit(solution)/shard_map/all_to_all | solution.py:28
  516.0 2.3 collective-permute-start.3
  518.3 12.7 all-to-all-done
  533.9 568.5 %all-reduce.5.cloned.1.call-done = (f32[128,1024]{0,1:T(8,128)}, f32[1024,128]{1,0:T(8,128)}) async-done(((f32[128,1024]{0,1:T(8,128)}, f32[1024,128]{1,0:T(8,128)}), (f32[128,1024]{0,1:T(8,128)}, f32[1024,128]{1,0:T(8,128)})) %all-reduce.5.cloned.1.call-update) | async-done | bytes 1048592 | tf_op jit(solution)/shard_map/psum | solution.py:93
  1103.1 132.1 %psum.44 = f32[1024]{0:T(1024)S(1)} all-reduce(f32[1024]{0:T(1024)S(1)} %get-tuple-element.249), channel_id=1, replica_groups=mesh['blk'=64,'row'=8] {'blk'}, use_global_device_ids=true, to_apply=%region_12.13 | all-reduce | flops 1024 | bytes 8192 | tf_op jit(solution)/shard_map/psum | solution.py:93
  1235.2 83.1 %psum.45 = f32[1024]{0:T(1024)S(1)} all-reduce(f32[1024]{0:T(1024)S(1)} %psum.44), channel_id=1, replica_groups=mesh['blk'=64,'row'=8] {'row'}, use_global_device_ids=true, to_apply=%region_13.14 | all-reduce | flops 1024 | bytes 8192 | tf_op jit(solution)/shard_map/psum | solution.py:92
  (506 shorter events, 296.4 us)
Async XLA Ops:
  35.1 14.2 %collective-permute-start = (bf16[128,128]{1,0:T(8,128)(2,1)S(1)}, bf16[128,128]{1,0:T(8,128)(2,1)S(1)}, u32[]{:S(2)}, u32[]{:S(2)}) collective-permute-start(bf16[128,128]{1,0:T(8,128)(2,1)S(1)} %get-tuple-element.332), channel_id=1, source_target_pairs={{0,8},{8,16},{16,24},{24,32},{32,40},{40,48},{48,56},{56,64},{64,7... | collective-permute-start | bytes 98312 | tf_op jit(solution)/shard_map/while/body/eval_jaxpr/ppermute | solution.py:17
  38.0 13.2 collective-permute-start.1
  41.2 12.7 collective-permute-start.2
  54.1 8.9 collective-permute-start
  56.0 8.9 collective-permute-start.1
  58.0 9.4 collective-permute-start.2
  67.7 8.9 collective-permute-start
  69.6 8.9 collective-permute-start.1
  71.5 9.8 collective-permute-start.2
  85.5 9.4 collective-permute-start.2
  97.1 8.9 collective-permute-start.1
  99.0 9.6 collective-permute-start.2
  108.8 8.9 collective-permute-start
  110.8 8.9 collective-permute-start.1
  112.7 9.4 collective-permute-start.2
  122.4 8.9 collective-permute-start
  124.3 8.9 collective-permute-start.1
  126.3 9.4 collective-permute-start.2
  135.9 8.9 collective-permute-start
  139.8 9.4 collective-permute-start.2
  149.5 8.9 collective-permute-start
  151.4 8.9 collective-permute-start.1
  153.4 9.4 collective-permute-start.2
  163.0 8.9 collective-permute-start
  165.0 8.9 collective-permute-start.1
  166.9 9.4 collective-permute-start.2
  180.4 9.4 collective-permute-start.2
  190.1 8.9 collective-permute-start
  192.0 9.5 collective-permute-start.1
  194.0 10.1 collective-permute-start.2
  204.3 9.2 collective-permute-start
  206.2 8.9 collective-permute-start.1
  208.2 9.4 collective-permute-start.2
  217.8 8.9 collective-permute-start
  219.8 8.9 collective-permute-start.1
  221.7 9.5 collective-permute-start.2
  235.3 9.4 collective-permute-start.2
  246.9 9.4 collective-permute-start.1
  248.9 9.9 collective-permute-start.2
  259.1 8.9 collective-permute-start
  261.0 8.9 collective-permute-start.1
  263.0 9.4 collective-permute-start.2
  276.5 9.6 collective-permute-start.2
  290.2 9.4 collective-permute-start.2
  303.7 9.4 collective-permute-start.2
  317.3 9.4 collective-permute-start.2
  330.8 9.4 collective-permute-start.2
  344.4 9.4 collective-permute-start.2
  354.1 9.5 collective-permute-start
  357.9 9.4 collective-permute-start.2
  371.5 9.4 collective-permute-start.2
  381.1 9.2 collective-permute-start
  385.0 9.4 collective-permute-start.2
  398.6 9.5 collective-permute-start.2
  412.2 9.4 collective-permute-start.2
  423.8 9.4 collective-permute-start.1
  425.7 9.9 collective-permute-start.2
  439.8 9.4 collective-permute-start.2
  453.3 9.6 collective-permute-start.2
  467.0 9.4 collective-permute-start.2
  476.7 54.4 %all-to-all-start = ((f32[8,128,128]{2,1,0:T(8,128)}), f32[8,128,128]{2,1,0:T(8,128)S(1)}, u32[]{:S(2)}, u32[]{:S(2)}) async-start(f32[8,128,128]{2,1,0:T(8,128)} %bitcast), calls=%async_computation | async-start | bytes 1048576 | tf_op jit(solution)/shard_map/all_to_all | solution.py:28
  515.9 586.4 %all-reduce.5.cloned.1.call-start = ((), (), s32[]{:S(2)}) async-start(), calls=%async_computation.1 | async-start | bytes 2097152 | tf_op jit(solution)/shard_map/psum | solution.py:93
  516.0 15.2 %collective-permute-start.3 = (f32[128,128]{0,1:T(8,128)S(1)}, f32[128,128]{0,1:T(8,128)S(1)}, u32[]{:S(2)}, u32[]{:S(2)}) collective-permute-start(f32[128,128]{0,1:T(8,128)S(1)} %copy.30), channel_id=1, source_target_pairs={{0,256},{8,264},{16,272},{24,280},{32,288},{40,296},{48,304},{56,3... | collective-permute-start | bytes 196616 | tf_op jit(solution)/shard_map/ppermute | solution.py:17
  533.8 785.0 %all-reduce.7.cloned.1.call-start = ((), (), s32[]{:S(2)}) async-start(), calls=%async_computation.2 | async-start | bytes 2097152 | tf_op jit(solution)/shard_map/psum | solution.py:92
  (43 other events, 327.8 us)
Sparse Core Ops, SparseCore 0:
  534.0 568.3 all-reduce.4
  1105.3 123.1 all-reduce.6
